TPU v7x, 32 devices: a whole 2x2x4 slice. The times are simulated.
32 devices in a mesh: dp: 4 (over z), fsdp: 8 (over y, x, core).
Axes of the slice: x: 2, y: 2, z: 4, core: 2. Of those that a mesh axis runs over, the one named last changes fastest.
Arguments:
- tokens: bfloat16 [4096, 1280], P(('dp', 'fsdp')), may hold values from -6 to 6
- lengths: int32 [32, 2], P(('dp', 'fsdp')), may hold values from 1 to 96, 128 in all within a row
- padding: int32 [4096], P(('dp', 'fsdp')), may hold values 0 or 1
- ln1_gain: bfloat16 [1280], P('fsdp'), may hold values from 0.099609375 to 1.8984375
- ln1_bias: bfloat16 [1280], P('fsdp'), may hold values from -4 to 4
- w_qkv: bfloat16 [1280, 3840], P('fsdp'), may hold values from -0.15625 to 0.15625
- b_query: bfloat16 [1280], P('fsdp'), may hold values from -4 to 4
- b_value: bfloat16 [1280], P('fsdp'), may hold values from -4 to 4
- w_out: bfloat16 [1280, 1280], P('fsdp'), may hold values from -0.625 to 0.625
- b_out: bfloat16 [1280], P('fsdp'), may hold values from -4 to 4
- ln2_gain: bfloat16 [1280], P('fsdp'), may hold values from 0.099609375 to 1.8984375
- ln2_bias: bfloat16 [1280], P('fsdp'), may hold values from -4 to 4
- w_up: bfloat16 [1280, 5120], P('fsdp'), may hold values from -0.15625 to 0.15625
- b_up: bfloat16 [5120], P('fsdp'), may hold values from -6 to 6
- w_down: bfloat16 [5120, 1280], P('fsdp'), may hold values from -0.078125 to 0.078125
- b_down: bfloat16 [1280], P('fsdp'), may hold values from -4 to 4
- cotangent: bfloat16 [4096, 1280], P(('dp', 'fsdp')), may hold values from -6 to 6
Outputs:
- layer_out: bfloat16 [4096, 1280], P(('dp', 'fsdp'))
- grad_tokens: float32 [4096, 1280], P(('dp', 'fsdp'))
- grad_ln1_gain: float32 [1280], P('fsdp')
- grad_ln1_bias: float32 [1280], P('fsdp')
- grad_w_qkv: float32 [1280, 3840], P('fsdp')
- grad_b_query: float32 [1280], P('fsdp')
- grad_b_value: float32 [1280], P('fsdp')
- grad_w_out: float32 [1280, 1280], P('fsdp')
- grad_b_out: float32 [1280], P('fsdp')
- grad_ln2_gain: float32 [1280], P('fsdp')
- grad_ln2_bias: float32 [1280], P('fsdp')
- grad_w_up: float32 [1280, 5120], P('fsdp')
- grad_b_up: float32 [5120], P('fsdp')
- grad_w_down: float32 [5120, 1280], P('fsdp')
- grad_b_down: float32 [1280], P('fsdp')
- cls_mean: float32 [1280], replicated
- cls_var: float32 [1280], replicated
Inputs may be any that keep to these rules, and one draw needn't show every extreme that they name: `lengths`: each row sums to 128; each length lies between 32 and 96. `padding`: A CLS token is a key whatever its mark.
All inputs are finite; a program needn't handle non-finite values. No bound on the sum of `padding` on one device may be relied on, other than what follows from the above.
Results may differ from a plain program's by a relative error of at most 0.015.
Values may be sent and summed in bfloat16 or wider, within the bound.
No kernel may reach another device: no remote copies, remote signals or barrier semaphores. Data moves between devices by JAX's collectives and lax.ppermute only.
A program may use at most 256 MiB of HBM per device.

v0:
```python
from functools import partial
import jax
import jax.numpy as jnp
from jax import lax
from jax.sharding import PartitionSpec as P

D = 1280
HEADS = 20
HEAD_DIM = 64
CELLS_DEV = 2
EPS = 1e-05


def norm_forward(values, norm_gain, norm_bias):
    center = jnp.mean(values, axis=-1, keepdims=True)
    centred = values - center
    spread = jnp.mean(centred * centred, axis=-1, keepdims=True)
    inverse = lax.rsqrt(spread + EPS)
    normed = centred * inverse
    return (normed * norm_gain + norm_bias, normed, inverse)


def norm_backward(grad_out, normed, inverse, norm_gain):
    grad_normed = grad_out * norm_gain
    first_mean = jnp.mean(grad_normed, axis=-1, keepdims=True)
    second_mean = jnp.mean(grad_normed * normed, axis=-1, keepdims=True)
    grad_in = inverse * (grad_normed - first_mean - normed * second_mean)
    return (grad_in, jnp.sum(grad_out * normed, axis=0), jnp.sum(grad_out, axis=0))


def cell_layout(lengths_row, padding_row):
    places = jnp.arange(padding_row.shape[0], dtype=jnp.int32)
    finish = jnp.cumsum(lengths_row)
    starts = finish - lengths_row
    member = jnp.sum((places[:, None] >= finish[None, :]).astype(jnp.int32), axis=1)
    leading = jnp.any(places[:, None] == starts[None, :], axis=1)
    usable = (padding_row > 0) | leading
    allowed = (member[:, None] == member[None, :]) & usable[None, :]
    return (allowed, leading)


def masked_scores(query_low, key_low, allowed, score_scale):
    raw = jnp.einsum("thd,shd->hts", query_low, key_low, preferred_element_type=jnp.float32)
    return jnp.where(allowed[None], raw * score_scale, -1e30)


def reduce_late(values):
    owned = (
        lax.psum_scatter(values[0], "fsdp", scatter_dimension=0, tiled=True),
        lax.psum_scatter(values[1], "fsdp", scatter_dimension=0, tiled=True),
        lax.psum_scatter(values[2], "fsdp", scatter_dimension=0, tiled=True),
        lax.psum_scatter(values[3], "fsdp", scatter_dimension=0, tiled=True),
        lax.psum_scatter(values[4], "fsdp", scatter_dimension=0, tiled=True),
        lax.psum_scatter(values[5], "fsdp", scatter_dimension=0, tiled=True),
        lax.psum_scatter(values[6], "fsdp", scatter_dimension=0, tiled=True),
        lax.psum_scatter(values[7], "fsdp", scatter_dimension=0, tiled=True),
        lax.psum_scatter(values[8], "fsdp", scatter_dimension=0, tiled=True),
        lax.psum_scatter(values[9], "fsdp", scatter_dimension=0, tiled=True),
        lax.psum_scatter(values[10], "fsdp", scatter_dimension=0, tiled=True),
        lax.psum_scatter(values[11], "fsdp", scatter_dimension=0, tiled=True),
        lax.psum_scatter(values[12], "fsdp", scatter_dimension=0, tiled=True),
    )
    shares = (
        lax.psum_scatter(
            owned[0].astype(jnp.bfloat16), "dp", scatter_dimension=0, tiled=True
        ).astype(jnp.float32),
        lax.psum_scatter(
            owned[1].astype(jnp.bfloat16), "dp", scatter_dimension=0, tiled=True
        ).astype(jnp.float32),
        lax.psum_scatter(
            owned[2].astype(jnp.bfloat16), "dp", scatter_dimension=0, tiled=True
        ).astype(jnp.float32),
        lax.psum_scatter(
            owned[3].astype(jnp.bfloat16), "dp", scatter_dimension=0, tiled=True
        ).astype(jnp.float32),
        lax.psum_scatter(
            owned[4].astype(jnp.bfloat16), "dp", scatter_dimension=0, tiled=True
        ).astype(jnp.float32),
        lax.psum_scatter(
            owned[5].astype(jnp.bfloat16), "dp", scatter_dimension=0, tiled=True
        ).astype(jnp.float32),
        lax.psum_scatter(
            owned[6].astype(jnp.bfloat16), "dp", scatter_dimension=0, tiled=True
        ).astype(jnp.float32),
        lax.psum_scatter(
            owned[7].astype(jnp.bfloat16), "dp", scatter_dimension=0, tiled=True
        ).astype(jnp.float32),
        lax.psum_scatter(
            owned[8].astype(jnp.bfloat16), "dp", scatter_dimension=0, tiled=True
        ).astype(jnp.float32),
        lax.psum_scatter(
            owned[9].astype(jnp.bfloat16), "dp", scatter_dimension=0, tiled=True
        ).astype(jnp.float32),
        lax.psum_scatter(
            owned[10].astype(jnp.bfloat16), "dp", scatter_dimension=0, tiled=True
        ).astype(jnp.float32),
        lax.psum_scatter(
            owned[11].astype(jnp.bfloat16), "dp", scatter_dimension=0, tiled=True
        ).astype(jnp.float32),
        lax.psum_scatter(
            owned[12].astype(jnp.bfloat16), "dp", scatter_dimension=0, tiled=True
        ).astype(jnp.float32),
    )
    return (
        lax.all_gather(shares[0].astype(jnp.bfloat16), "dp", axis=0, tiled=True).astype(
            jnp.float32
        ),
        lax.all_gather(shares[1].astype(jnp.bfloat16), "dp", axis=0, tiled=True).astype(
            jnp.float32
        ),
        lax.all_gather(shares[2].astype(jnp.bfloat16), "dp", axis=0, tiled=True).astype(
            jnp.float32
        ),
        lax.all_gather(shares[3].astype(jnp.bfloat16), "dp", axis=0, tiled=True).astype(
            jnp.float32
        ),
        lax.all_gather(shares[4].astype(jnp.bfloat16), "dp", axis=0, tiled=True).astype(
            jnp.float32
        ),
        lax.all_gather(shares[5].astype(jnp.bfloat16), "dp", axis=0, tiled=True).astype(
            jnp.float32
        ),
        lax.all_gather(shares[6].astype(jnp.bfloat16), "dp", axis=0, tiled=True).astype(
            jnp.float32
        ),
        lax.all_gather(shares[7].astype(jnp.bfloat16), "dp", axis=0, tiled=True).astype(
            jnp.float32
        ),
        lax.all_gather(shares[8].astype(jnp.bfloat16), "dp", axis=0, tiled=True).astype(
            jnp.float32
        ),
        lax.all_gather(shares[9].astype(jnp.bfloat16), "dp", axis=0, tiled=True).astype(
            jnp.float32
        ),
        lax.all_gather(shares[10].astype(jnp.bfloat16), "dp", axis=0, tiled=True).astype(
            jnp.float32
        ),
        lax.all_gather(shares[11].astype(jnp.bfloat16), "dp", axis=0, tiled=True).astype(
            jnp.float32
        ),
        lax.all_gather(shares[12].astype(jnp.bfloat16), "dp", axis=0, tiled=True).astype(
            jnp.float32
        ),
    )


def local(
    tokens,
    lengths,
    padding,
    ln1_gain,
    ln1_bias,
    w_qkv,
    b_query,
    b_value,
    w_out,
    b_out,
    ln2_gain,
    ln2_bias,
    w_up,
    b_up,
    w_down,
    b_down,
    cotangent,
):
    fsdp_count = lax.axis_size("fsdp")
    dp_count = lax.axis_size("dp")
    f32 = jnp.float32
    bf16 = jnp.bfloat16
    row_total = tokens.shape[0]
    score_scale = HEAD_DIM ** (-0.5)
    (
        first_gain,
        first_bias,
        whole_qkv,
        query_bias,
        value_bias,
        whole_out,
        out_bias,
        second_gain,
        second_bias,
        whole_up,
        up_bias,
        whole_down,
        down_bias,
    ) = (
        lax.all_gather(ln1_gain, "fsdp", axis=0, tiled=True),
        lax.all_gather(ln1_bias, "fsdp", axis=0, tiled=True),
        lax.all_gather(w_qkv, "fsdp", axis=0, tiled=True),
        lax.all_gather(b_query, "fsdp", axis=0, tiled=True),
        lax.all_gather(b_value, "fsdp", axis=0, tiled=True),
        lax.all_gather(w_out, "fsdp", axis=0, tiled=True),
        lax.all_gather(b_out, "fsdp", axis=0, tiled=True),
        lax.all_gather(ln2_gain, "fsdp", axis=0, tiled=True),
        lax.all_gather(ln2_bias, "fsdp", axis=0, tiled=True),
        lax.all_gather(w_up, "fsdp", axis=0, tiled=True),
        lax.all_gather(b_up, "fsdp", axis=0, tiled=True),
        lax.all_gather(w_down, "fsdp", axis=0, tiled=True),
        lax.all_gather(b_down, "fsdp", axis=0, tiled=True),
    )
    allowed, leading = cell_layout(lengths[0], padding)
    inputs = tokens.astype(f32)
    first_out, first_normed, first_inverse = norm_forward(
        inputs, first_gain.astype(f32), first_bias.astype(f32)
    )
    first_low = first_out.astype(bf16)
    projected = jnp.dot(first_low, whole_qkv, preferred_element_type=f32)
    query_low = (
        (projected[:, :D] + query_bias.astype(f32)).astype(bf16).reshape(row_total, HEADS, HEAD_DIM)
    )
    key_low = projected[:, D : 2 * D].astype(bf16).reshape(row_total, HEADS, HEAD_DIM)
    value_low = (
        (projected[:, 2 * D :] + value_bias.astype(f32))
        .astype(bf16)
        .reshape(row_total, HEADS, HEAD_DIM)
    )
    masked = masked_scores(query_low, key_low, allowed, score_scale)
    top_score = jnp.max(masked, axis=-1, keepdims=True)
    log_total = top_score + jnp.log(jnp.sum(jnp.exp(masked - top_score), axis=-1, keepdims=True))
    probs_low = jnp.exp(masked - log_total).astype(bf16)
    context = jnp.einsum("hts,shd->thd", probs_low, value_low, preferred_element_type=f32)
    context_low = context.reshape(row_total, D).astype(bf16)
    mixed = (
        inputs + jnp.dot(context_low, whole_out, preferred_element_type=f32) + out_bias.astype(f32)
    )
    second_out, second_normed, second_inverse = norm_forward(
        mixed, second_gain.astype(f32), second_bias.astype(f32)
    )
    second_low = second_out.astype(bf16)
    hidden_pre = jnp.dot(second_low, whole_up, preferred_element_type=f32) + up_bias.astype(f32)
    activated, gelu_pull = jax.vjp(partial(jax.nn.gelu, approximate=False), hidden_pre)
    act_low = activated.astype(bf16)
    result = (
        mixed + jnp.dot(act_low, whole_down, preferred_element_type=f32) + down_bias.astype(f32)
    )
    picked = jnp.where(leading[:, None], result, 0.0)
    moment_sum, moment_square = lax.psum(
        (jnp.sum(picked, axis=0), jnp.sum(picked * picked, axis=0)), ("dp", "fsdp")
    )
    cell_total = CELLS_DEV * dp_count * fsdp_count
    cls_mean = moment_sum / cell_total
    cls_var = moment_square / cell_total - cls_mean * cls_mean
    (
        first_gain,
        first_bias,
        whole_qkv,
        query_bias,
        value_bias,
        whole_out,
        out_bias,
        second_gain,
        second_bias,
        whole_up,
        up_bias,
        whole_down,
        down_bias,
    ) = (
        lax.all_gather(ln1_gain, "fsdp", axis=0, tiled=True),
        lax.all_gather(ln1_bias, "fsdp", axis=0, tiled=True),
        lax.all_gather(w_qkv, "fsdp", axis=0, tiled=True),
        lax.all_gather(b_query, "fsdp", axis=0, tiled=True),
        lax.all_gather(b_value, "fsdp", axis=0, tiled=True),
        lax.all_gather(w_out, "fsdp", axis=0, tiled=True),
        lax.all_gather(b_out, "fsdp", axis=0, tiled=True),
        lax.all_gather(ln2_gain, "fsdp", axis=0, tiled=True),
        lax.all_gather(ln2_bias, "fsdp", axis=0, tiled=True),
        lax.all_gather(w_up, "fsdp", axis=0, tiled=True),
        lax.all_gather(b_up, "fsdp", axis=0, tiled=True),
        lax.all_gather(w_down, "fsdp", axis=0, tiled=True),
        lax.all_gather(b_down, "fsdp", axis=0, tiled=True),
    )
    grad_result = cotangent.astype(f32)
    grad_down_bias = jnp.sum(grad_result, axis=0)
    grad_whole_down = jnp.einsum("tf,td->fd", act_low, cotangent, preferred_element_type=f32)
    grad_act = jnp.einsum("td,fd->tf", cotangent, whole_down, preferred_element_type=f32)
    grad_pre = gelu_pull(grad_act)[0].astype(bf16)
    grad_up_bias = jnp.sum(grad_pre.astype(f32), axis=0)
    grad_whole_up = jnp.einsum("td,tf->df", second_low, grad_pre, preferred_element_type=f32)
    grad_second = jnp.einsum("tf,df->td", grad_pre, whole_up, preferred_element_type=f32)
    grad_from_second, grad_second_gain, grad_second_bias = norm_backward(
        grad_second, second_normed, second_inverse, second_gain.astype(f32)
    )
    grad_mixed = grad_result + grad_from_second
    grad_branch = grad_mixed.astype(bf16)
    grad_out_bias = jnp.sum(grad_branch.astype(f32), axis=0)
    grad_whole_out = jnp.einsum("td,te->de", context_low, grad_branch, preferred_element_type=f32)
    grad_context = jnp.einsum("te,de->td", grad_branch, whole_out, preferred_element_type=f32)
    grad_context = grad_context.astype(bf16).reshape(row_total, HEADS, HEAD_DIM)
    masked = masked_scores(query_low, key_low, allowed, score_scale)
    probs = jnp.exp(masked - log_total)
    probs_low = probs.astype(bf16)
    grad_probs = jnp.einsum("thd,shd->hts", grad_context, value_low, preferred_element_type=f32)
    along = jnp.sum(grad_probs * probs, axis=-1, keepdims=True)
    grad_scores = (probs * (grad_probs - along) * score_scale).astype(bf16)
    grad_value = jnp.einsum(
        "hts,thd->shd", probs_low, grad_context, preferred_element_type=f32
    ).astype(bf16)
    grad_query = jnp.einsum(
        "hts,shd->thd", grad_scores, key_low, preferred_element_type=f32
    ).astype(bf16)
    grad_key = jnp.einsum(
        "hts,thd->shd", grad_scores, query_low, preferred_element_type=f32
    ).astype(bf16)
    grad_query = grad_query.reshape(row_total, D)
    grad_key = grad_key.reshape(row_total, D)
    grad_value = grad_value.reshape(row_total, D)
    grad_query_bias = jnp.sum(grad_query.astype(f32), axis=0)
    grad_value_bias = jnp.sum(grad_value.astype(f32), axis=0)
    grad_projected = jnp.concatenate([grad_query, grad_key, grad_value], axis=1)
    grad_whole_qkv = jnp.einsum("td,te->de", first_low, grad_projected, preferred_element_type=f32)
    grad_first = jnp.einsum("te,de->td", grad_projected, whole_qkv, preferred_element_type=f32)
    grad_from_first, grad_first_gain, grad_first_bias = norm_backward(
        grad_first, first_normed, first_inverse, first_gain.astype(f32)
    )
    grad_inputs = grad_mixed + grad_from_first
    totals = reduce_late(
        (
            grad_first_gain,
            grad_first_bias,
            grad_whole_qkv,
            grad_query_bias,
            grad_value_bias,
            grad_whole_out,
            grad_out_bias,
            grad_second_gain,
            grad_second_bias,
            grad_whole_up,
            grad_up_bias,
            grad_whole_down,
            grad_down_bias,
        )
    )
    return (
        result.astype(bf16),
        grad_inputs,
        totals[0],
        totals[1],
        totals[2],
        totals[3],
        totals[4],
        totals[5],
        totals[6],
        totals[7],
        totals[8],
        totals[9],
        totals[10],
        totals[11],
        totals[12],
        cls_mean,
        cls_var,
    )


def solution(mesh):
    in_specs = (
        P(("dp", "fsdp"), None),
        P(("dp", "fsdp"), None),
        P(("dp", "fsdp")),
        P("fsdp"),
        P("fsdp"),
        P("fsdp", None),
        P("fsdp"),
        P("fsdp"),
        P("fsdp", None),
        P("fsdp"),
        P("fsdp"),
        P("fsdp"),
        P("fsdp", None),
        P("fsdp"),
        P("fsdp", None),
        P("fsdp"),
        P(("dp", "fsdp"), None),
    )
    out_specs = (
        P(("dp", "fsdp"), None),
        P(("dp", "fsdp"), None),
        P("fsdp"),
        P("fsdp"),
        P("fsdp", None),
        P("fsdp"),
        P("fsdp"),
        P("fsdp", None),
        P("fsdp"),
        P("fsdp"),
        P("fsdp"),
        P("fsdp", None),
        P("fsdp"),
        P("fsdp", None),
        P("fsdp"),
        P(),
        P(),
    )
    return jax.shard_map(local, mesh=mesh, in_specs=in_specs, out_specs=out_specs, check_vma=False)
```

profile of v0, /device:TPU:0, one launch (start us, length us, event | category | flops | bytes accessed | tf_op | source)
XLA Modules:
  0.0 1096.7 jit_solution(2530237779539740819)
XLA Ops:
  7.4 0.7 all-gather.9.cloned.1.call-update
  8.1 0.7 all-gather.11.cloned.1.call-update
  8.9 0.7 all-gather.13.cloned.1.call-update
  9.6 0.5 all-gather.15.cloned.1.call-update
  10.3 0.6 fusion.70
  13.5 25.9 %all-reduce.37 = (bf16[1280]{0:T(1024)(128)(2,1)S(1)}, bf16[1280]{0:T(1024)(128)(2,1)S(1)}, bf16[1280]{0:T(1024)(128)(2,1)S(1)}, bf16[1280]{0:T(1024)(128)(2,1)S...) all-reduce(bf16[1280]{0:T(1024)(128)(2,1)S(1)} %dynamic-update-slic, ...), channel_id=1, replica_groups=mesh['dp'=4,'fsdp'=8] {'fsdp'}, use_global_device_ids=true, to_apply=%add.1 | all-reduce | flops 10240 | bytes 40960
  39.5 8.1 all-gather
  48.6 24.9 %all-gather.9.cloned.1.call-done = bf16[1280,3840]{1,0:T(8,128)(2,1)} async-done(((bf16[160,3840]{1,0:T(8,128)(2,1)}), bf16[1280,3840]{1,0:T(8,128)(2,1)}) %all-gather.9.cloned.1.call-update) | async-done | bytes 9830416 | tf_op jit(solution)/shard_map/all_gather | solution.py:189
  73.4 5.3 fusion.66
  80.2 0.8 copy-done.1
  81.4 26.8 %all-gather.11.cloned.1.call-done = bf16[1280,1280]{1,0:T(8,128)(2,1)} async-done(((bf16[160,1280]{1,0:T(8,128)(2,1)}), bf16[1280,1280]{1,0:T(8,128)(2,1)}) %all-gather.11.cloned.1.call-update) | async-done | bytes 3276816 | tf_op jit(solution)/shard_map/all_gather | solution.py:192
  108.2 2.7 fusion.73
  111.1 73.4 %all-gather.13.cloned.1.call-done = bf16[1280,5120]{1,0:T(8,128)(2,1)} async-done(((bf16[160,5120]{1,0:T(8,128)(2,1)}), bf16[1280,5120]{1,0:T(8,128)(2,1)}) %all-gather.13.cloned.1.call-update) | async-done | bytes 13107216 | tf_op jit(solution)/shard_map/all_gather | solution.py:196
  184.5 8.2 convolution_add_fusion
  192.7 67.9 %all-gather.15.cloned.1.call-done = bf16[5120,1280]{1,0:T(8,128)(2,1)} async-done(((bf16[640,1280]{1,0:T(8,128)(2,1)}), bf16[5120,1280]{1,0:T(8,128)(2,1)}) %all-gather.15.cloned.1.call-update) | async-done | bytes 13107216 | tf_op jit(solution)/shard_map/all_gather | solution.py:198
  260.6 14.4 %convert_reduce_fusion = (f32[5120]{0:T(1024)S(1)}, bf16[128,5120]{1,0:T(8,128)(2,1)}, f32[128,5120]{1,0:T(8,128)}) fusion(f32[128,5120]{1,0:T(8,128)} %convolution_add_fusion, bf16[128,1280]{1,0:T(8,128)(2,1)} %param.33, bf16[5120,1280]{1,0:T(8,128)(2,1)} %all-gather.15.cloned.1.call-done), kind=kOutput, calls=%fused_computation.4 | convolution fusion | flops 1726213120 | bytes 20008960 | tf_op jit(solution)/shard_map/td,fd->tf/dot_general | solution.py:275
  275.1 6.6 multiply_reduce_fusion.2
  281.7 1.5 convert_reduce_fusion.3
  283.2 4.0 convolution_convert_fusion
  287.2 1.9 copy.66
  289.1 2.3 convert_reduce_fusion.4
  291.3 2.5 fusion.76
  293.8 3.1 fusion.24
  296.9 3.1 convert_reduce_fusion.5
  300.0 9.3 fusion.50
  309.4 1.2 copy-done.4
  310.6 15.4 %fusion.68 = f32[1280,5120]{1,0:T(8,128)} fusion(bf16[128,5120]{1,0:T(8,128)(2,1)S(1)} %copy-done.4, f32[128,1280]{1,0:T(8,128)S(1)} %get-tuple-element.82, f32[1280]{0:T(1024)S(1)} %convert_element_type.233, f32[1280]{0:T(1024)S(1)} %convert_element_type.232, f32[128]{0:T(128)S(1)} %add_rsqrt_fusion, f32[128]{0:T(128)S(1)} %broadcast_multiply_fusion.5), kind=kOutput, calls=%fused_computation.121 | convolution fusion | flops 1678540800 | bytes 28191744 | tf_op jit(solution)/shard_map/td,tf->df/dot_general | solution.py:278
  326.1 4.1 multiply_convert_fusion
  330.2 12.7 %fusion.77 = f32[5120,1280]{1,0:T(8,128)} fusion(bf16[128,5120]{1,0:T(8,128)(2,1)S(1)} %multiply_convert_fusion, bf16[128,1280]{1,0:T(8,128)(2,1)S(1)} %copy-done.8), kind=kOutput, calls=%fused_computation.127 | convolution fusion | flops 1677721600 | bytes 27852800 | tf_op jit(solution)/shard_map/tf,td->fd/dot_general | solution.py:274
  342.9 3.8 fusion.60
  346.8 92.3 %reduce-scatter.9.cloned.1.call-done = f32[160,3840]{1,0:T(8,128)} async-done(((f32[1280,3840]{1,0:T(8,128)}), f32[160,3840]{1,0:T(8,128)}) %reduce-scatter.9.cloned.1.call-update) | async-done | bytes 2457616 | tf_op jit(solution)/shard_map/reduce_scatter | solution.py:51
  439.2 2.8 convert_element_type.254
  442.1 163.0 %reduce-scatter.17.cloned.1.call-done = f32[160,5120]{1,0:T(8,128)} async-done(((f32[1280,5120]{1,0:T(8,128)}), f32[160,5120]{1,0:T(8,128)}) %reduce-scatter.17.cloned.1.call-update) | async-done | bytes 3276816 | tf_op jit(solution)/shard_map/reduce_scatter | solution.py:58
  605.1 3.3 convert_element_type.271
  608.5 162.7 %reduce-scatter.21.cloned.1.call-done = f32[640,1280]{1,0:T(8,128)} async-done(((f32[5120,1280]{1,0:T(8,128)}), f32[640,1280]{1,0:T(8,128)}) %reduce-scatter.21.cloned.1.call-update) | async-done | bytes 3276816 | tf_op jit(solution)/shard_map/reduce_scatter | solution.py:60
  771.1 3.2 convert_element_type.276
  774.5 63.1 %reduce-scatter.13.cloned.1.call-done = f32[160,1280]{1,0:T(8,128)} async-done(((f32[1280,1280]{1,0:T(8,128)}), f32[160,1280]{1,0:T(8,128)}) %reduce-scatter.13.cloned.1.call-update) | async-done | bytes 819216 | tf_op jit(solution)/shard_map/reduce_scatter | solution.py:54
  837.6 1.9 convert_element_type.262
  839.6 31.1 %reduce-scatter.11.cloned.1.call-done = bf16[40,3840]{1,0:T(8,128)(2,1)} async-done(((bf16[160,3840]{1,0:T(8,128)(2,1)}), bf16[40,3840]{1,0:T(8,128)(2,1)}) %reduce-scatter.11.cloned.1.call-update) | async-done | bytes 307216 | tf_op jit(solution)/shard_map/reduce_scatter | solution.py:70
  870.8 37.8 %reduce-scatter.19.cloned.1.call-done = bf16[40,5120]{1,0:T(8,128)(2,1)} async-done(((bf16[160,5120]{1,0:T(8,128)(2,1)}), bf16[40,5120]{1,0:T(8,128)(2,1)}) %reduce-scatter.19.cloned.1.call-update) | async-done | bytes 409616 | tf_op jit(solution)/shard_map/reduce_scatter | solution.py:91
  912.6 34.4 %reduce-scatter.23.cloned.1.call-done = bf16[160,1280]{1,0:T(8,128)(2,1)} async-done(((bf16[640,1280]{1,0:T(8,128)(2,1)}), bf16[160,1280]{1,0:T(8,128)(2,1)}) %reduce-scatter.23.cloned.1.call-update) | async-done | bytes 409616 | tf_op jit(solution)/shard_map/reduce_scatter | solution.py:97
  947.0 8.2 fusion.40
  955.4 25.2 %all-reduce.36 = (bf16[1280]{0:T(1024)(128)(2,1)S(1)}, bf16[1280]{0:T(1024)(128)(2,1)S(1)}, bf16[1280]{0:T(1024)(128)(2,1)S(1)}, bf16[1280]{0:T(1024)(128)(2,1)S...) all-reduce(f32[1280]{0:T(1024)S(1)} %get-tuple-element.19, ...), channel_id=2, replica_groups=mesh['dp'=4,'fsdp'=8] {'fsdp'}, use_global_device_ids=true, to_apply=%region_15.16.clone | all-reduce | flops 15360 | bytes 92160
  981.3 10.8 all-reduce.39
  994.6 9.6 all-reduce.38
  1004.2 0.6 convert_element_type.251
  1004.8 0.6 convert_element_type.253
  1005.3 0.6 convert_element_type.258
  1005.9 0.6 convert_element_type.261
  1006.4 0.6 convert_element_type.266
  1007.0 0.6 convert_element_type.268
  1007.6 0.6 convert_element_type.270
  1008.1 0.6 convert_element_type.279
  1008.7 0.6 convert_element_type.275
  1009.3 7.6 multiply_reduce_fusion.1
  1016.9 40.5 %all-reduce.35 = (f32[1280]{0:T(1024)S(1)}, f32[1280]{0:T(1024)S(1)}) all-reduce(f32[1280]{0:T(1024)S(1)} %get-tuple-element.24, f32[1280]{0:T(1024)S(1)} %get-tuple-element.23), channel_id=1, replica_groups=mesh['dp'=4,'fsdp'=8] {'dp','fsdp'}, use_global_device_ids=true, to_apply=%region_50.51 | all-reduce | flops 2560 | bytes 20480 | tf_op jit(solution)/shard_map/psum | solution.py:237
  1057.3 0.6 multiply_subtract_fusion
  1058.0 2.2 fusion.39
  1060.1 18.6 %all_gather.102 = bf16[160,1280]{1,0:T(8,128)(2,1)S(1)} all-gather(bf16[40,1280]{1,0:T(8,128)(2,1)} %reduce-scatter.15.cloned.1.call-done), channel_id=1, replica_groups=mesh['dp'=4,'fsdp'=8] {'dp'}, dimensions={0}, use_global_device_ids=true | all-gather | bytes 512000 | tf_op jit(solution)/shard_map/all_gather | solution.py:120
  1078.7 0.9 convert_element_type.263
  1079.7 2.9 convert_element_type.255
  1082.5 3.5 convert_element_type.272
  1086.0 0.5 all-gather.21.cloned.1.call-done
  1086.5 3.4 convert_element_type.277
  (163 shorter events, 9.1 us)
Async XLA Ops:
  7.2 3.0 copy-start.10
  7.2 3.0 copy-start.11
  7.2 3.0 copy-start.12
  7.2 4.3 copy-start.13
  7.2 4.5 copy-start.14
  7.2 4.8 copy-start.15
  7.3 5.0 copy-start.16
  7.3 5.3 copy-start.17
  7.3 5.5 copy-start.18
  7.3 5.8 copy-start.19
  7.3 6.0 copy-start.20
  7.3 40.4 %copy-start.21 = (s32[1,2]{1,0:T(1,128)S(1)}, s32[1,2]{1,0:T(1,128)}, u32[]{:S(2)}) copy-start(s32[1,2]{1,0:T(1,128)} %param.18) | copy-start | bytes 28
  7.3 40.7 %copy-start.3 = (bf16[128,1280]{1,0:T(8,128)(2,1)S(1)}, bf16[128,1280]{1,0:T(8,128)(2,1)}, u32[]{:S(2)}) copy-start(bf16[128,1280]{1,0:T(8,128)(2,1)} %param.17) | copy-start | bytes 983044
  7.3 66.1 %all-gather.9.cloned.1.call-start = ((), (), s32[]{:S(2)}) async-start(), calls=%async_computation.8 | async-start | bytes 11059200 | tf_op jit(solution)/shard_map/all_gather | solution.py:189
  8.1 40.4 %copy-start.22 = (s32[128]{0:T(128)S(1)}, s32[128]{0:T(128)}, u32[]{:S(2)}) copy-start(s32[128]{0:T(128)} %param.19) | copy-start | bytes 1540
  8.1 100.2 %all-gather.11.cloned.1.call-start = ((), (), s32[]{:S(2)}) async-start(), calls=%async_computation.9 | async-start | bytes 3686400 | tf_op jit(solution)/shard_map/all_gather | solution.py:192
  8.8 175.7 %all-gather.13.cloned.1.call-start = ((), (), s32[]{:S(2)}) async-start(), calls=%async_computation.10 | async-start | bytes 14745600 | tf_op jit(solution)/shard_map/all_gather | solution.py:196
  9.6 251.1 %all-gather.15.cloned.1.call-start = ((), (), s32[]{:S(2)}) async-start(), calls=%async_computation.11 | async-start | bytes 14745600 | tf_op jit(solution)/shard_map/all_gather | solution.py:198
  10.1 429.0 %reduce-scatter.9.cloned.1.call-start = ((), (), s32[]{:S(2)}) async-start(), calls=%async_computation.12 | async-start | bytes 22118400 | tf_op jit(solution)/shard_map/reduce_scatter | solution.py:51
  79.1 2.3 copy-start.7
  79.4 2.0 copy-start.6
  79.6 1.8 copy-start.5
  80.0 1.1 copy-start.1
  260.6 14.4 %copy-start = (bf16[1280,5120]{1,0:T(8,128)(2,1)S(1)}, bf16[1280,5120]{1,0:T(8,128)(2,1)}, u32[]{:S(2)}) copy-start(bf16[1280,5120]{1,0:T(8,128)(2,1)} %all-gather.13.cloned.1.call-done) | copy-start | bytes 39321604
  283.2 5.8 copy-start.2
  309.3 1.3 copy-start.4
  309.4 295.7 %reduce-scatter.17.cloned.1.call-start = ((), (), s32[]{:S(2)}) async-start(), calls=%async_computation.17 | async-start | bytes 29491200 | tf_op jit(solution)/shard_map/reduce_scatter | solution.py:58
  326.0 445.1 %reduce-scatter.21.cloned.1.call-start = ((), (), s32[]{:S(2)}) async-start(), calls=%async_computation.20 | async-start | bytes 29491200 | tf_op jit(solution)/shard_map/reduce_scatter | solution.py:60
  326.1 4.1 copy-start.8
  342.9 494.8 %reduce-scatter.13.cloned.1.call-start = ((), (), s32[]{:S(2)}) async-start(), calls=%async_computation.15 | async-start | bytes 7372800 | tf_op jit(solution)/shard_map/reduce_scatter | solution.py:54
  346.8 524.0 %reduce-scatter.11.cloned.1.call-start = ((), (), s32[]{:S(2)}) async-start(), calls=%async_computation.13 | async-start | bytes 1536000 | tf_op jit(solution)/shard_map/reduce_scatter | solution.py:70
  442.0 466.6 %reduce-scatter.19.cloned.1.call-start = ((), (), s32[]{:S(2)}) async-start(), calls=%async_computation.18 | async-start | bytes 2048000 | tf_op jit(solution)/shard_map/reduce_scatter | solution.py:91
  608.4 338.6 %reduce-scatter.23.cloned.1.call-start = ((), (), s32[]{:S(2)}) async-start(), calls=%async_computation.21 | async-start | bytes 2048000 | tf_op jit(solution)/shard_map/reduce_scatter | solution.py:97
  774.4 172.6 %copy-start.9 = (bf16[20,64,128]{2,1,0:T(8,128)(2,1)S(1)}, bf16[20,64,128]{2,1,0:T(8,128)(2,1)}, u32[]{:S(2)}) copy-start(bf16[20,64,128]{2,1,0:T(8,128)(2,1)} %get-tuple-element.89) | copy-start | bytes 983044
  774.4 285.7 %reduce-scatter.15.cloned.1.call-start = ((), (), s32[]{:S(2)}) async-start(), calls=%async_computation.16 | async-start | bytes 512000 | tf_op jit(solution)/shard_map/reduce_scatter | solution.py:79
  839.6 240.1 %all-gather.17.cloned.1.call-start = ((), (), s32[]{:S(2)}) async-start(), calls=%async_computation.14 | async-start | bytes 1536000 | tf_op jit(solution)/shard_map/all_gather | solution.py:111
  870.8 211.8 %all-gather.19.cloned.1.call-start = ((), (), s32[]{:S(2)}) async-start(), calls=%async_computation.19 | async-start | bytes 2048000 | tf_op jit(solution)/shard_map/all_gather | solution.py:132
  908.6 177.9 %all-gather.21.cloned.1.call-start = ((), (), s32[]{:S(2)}) async-start(), calls=%async_computation.22 | async-start | bytes 2048000 | tf_op jit(solution)/shard_map/all_gather | solution.py:138
Sparse Core Ops, SparseCore 0:
  10.0 63.3 all-gather.8
  75.3 32.8 all-gather.10
  110.1 74.3 all-gather.12
  186.2 74.3 all-gather.14
  309.5 129.6 reduce-scatter.8
  442.7 162.3 reduce-scatter.16
  608.8 162.3 reduce-scatter.20
  774.6 62.9 reduce-scatter.12
  840.6 30.0 reduce-scatter.10
  873.5 35.0 reduce-scatter.18
  911.6 35.3 reduce-scatter.22
  949.7 19.8 reduce-scatter.14
  971.2 30.5 all-gather.16
  1003.2 37.9 all-gather.18
  1042.8 43.7 all-gather.20
where the time goes:
time: 1100 us
  waiting for transfers between devices  781 us (71%)
  blocking collectives  139 us (13%)
  matrix products  110 us (10%)
  other arithmetic  36.9 us (3%)
  between operations  19.2 us (2%)
    reduce_scatter x1, waiting for transfers between devices, reduce_late(): lax.psum_scatter(values[9], 'fsdp', scatter_dimension=0, tiled=True)  163 us
    reduce_scatter x1, waiting for transfers between devices, reduce_late(): lax.psum_scatter(values[11], 'fsdp', scatter_dimension=0, tiled=True)  163 us
    reduce_scatter x1, waiting for transfers between devices, reduce_late(): lax.psum_scatter(values[2], 'fsdp', scatter_dimension=0, tiled=True)  92.3 us
    all_gather x1, waiting for transfers between devices, local(): lax.all_gather(w_up, 'fsdp', axis=0, tiled=True)  73.4 us
    unnamed x4, blocking collectives  71.4 us
    all_gather x1, waiting for transfers between devices, local(): lax.all_gather(w_down, 'fsdp', axis=0, tiled=True)  67.9 us
    reduce_scatter x1, waiting for transfers between devices, reduce_late(): lax.psum_scatter(values[5], 'fsdp', scatter_dimension=0, tiled=True)  63.1 us
    psum x1, blocking collectives, local(): lax.psum((jnp.sum(picked, axis=0), jnp.sum(picked * picked, axis=0)), ('d...  40.5 us
  transfers between devices with their start and end apart: 15, of which 12 were waited for; matrix products, arithmetic and copies ran while one was open for 9% of the time, Pallas kernels for 0%

commit v1 on v0

--- a/solution.py
+++ b/solution.py
@@ -1,3 +1,4 @@
+import functools
 from functools import partial
 import jax
 import jax.numpy as jnp
@@ -9,6 +10,22 @@
 HEAD_DIM = 64
 CELLS_DEV = 2
 EPS = 1e-05
+
+
+def positions_mark(panel, along_dim):
+    devs = lax.axis_size("fsdp")
+    items = [panel]
+    b = 1
+    while b < devs:
+        items.append(
+            lax.ppermute(items[b - 1], "fsdp", [(rr, (rr - 1) % devs) for rr in range(devs)])
+        )
+        b += 1
+    r_now = jnp.concatenate(items, along_dim)
+    return jnp.roll(r_now, lax.axis_index("fsdp") * panel.shape[along_dim], along_dim)
+
+
+link_routes_all = functools.partial(positions_mark, along_dim=0)
 
 
 def norm_forward(values, norm_gain, norm_bias):
@@ -189,7 +206,7 @@
         lax.all_gather(w_qkv, "fsdp", axis=0, tiled=True),
         lax.all_gather(b_query, "fsdp", axis=0, tiled=True),
         lax.all_gather(b_value, "fsdp", axis=0, tiled=True),
-        lax.all_gather(w_out, "fsdp", axis=0, tiled=True),
+        link_routes_all(w_out),
         lax.all_gather(b_out, "fsdp", axis=0, tiled=True),
         lax.all_gather(ln2_gain, "fsdp", axis=0, tiled=True),
         lax.all_gather(ln2_bias, "fsdp", axis=0, tiled=True),

time: 1100 us -> 1100 us (level)
  waiting for transfers between devices: 781 us -> 736 us
  starting transfers between devices: 0.6 us -> 19.6 us
  local copies, waits for them, and re-layouts: 10.8 us -> 23 us
    all_gather x1, waiting for transfers between devices: 73.4 us -> 21.7 us  [local(): lax.all_gather(w_up, 'fsdp', axis=0, tiled=True)]
    ppermute x0 -> x7, waiting for transfers between devices: none -> 46.7 us  [positions_mark(): lax.ppermute(items[b - 1], 'fsdp', [(rr, (rr - 1) % devs) for rr in range...]
    all_gather x1, waiting for transfers between devices: 24.9 us -> 0.01 us  [local(): lax.all_gather(w_qkv, 'fsdp', axis=0, tiled=True)]
    ppermute x0 -> x7, starting transfers between devices: none -> 19 us  [positions_mark(): lax.ppermute(items[b - 1], 'fsdp', [(rr, (rr - 1) % devs) for rr in range...]
    all_gather x1, waiting for transfers between devices: 26.8 us -> 12 us  [local(): lax.all_gather(w_out, 'fsdp', axis=0, tiled=True)]
    unnamed x100 -> x119, local copies, waits for them, and re-layouts: 8.09 us -> 19.6 us
  transfers between devices with their start and end apart: 15 -> 22, of which waited for: 12 -> 17; matrix products, arithmetic and copies ran while one was open for 9% -> 13% of each run, Pallas kernels for 0% -> 0%
where the time goes in v1:
time: 1100 us; the launch traced here: 1090 us
  waiting for transfers between devices  736 us (67%)
  blocking collectives  143 us (13%)
  matrix products  110 us (10%)
  other arithmetic  37 us (3%)
  local copies, waits for them, and re-layouts  23 us (2%)
  starting transfers between devices  19.6 us (2%)
  between operations  19.3 us (2%)
    reduce_scatter x1, waiting for transfers between devices, reduce_late(): lax.psum_scatter(values[9], 'fsdp', scatter_dimension=0, tiled=True)  163 us
    reduce_scatter x1, waiting for transfers between devices, reduce_late(): lax.psum_scatter(values[11], 'fsdp', scatter_dimension=0, tiled=True)  163 us
    reduce_scatter x1, waiting for transfers between devices, reduce_late(): lax.psum_scatter(values[2], 'fsdp', scatter_dimension=0, tiled=True)  92.4 us
    unnamed x4, blocking collectives  76.5 us
    all_gather x1, waiting for transfers between devices, local(): lax.all_gather(w_down, 'fsdp', axis=0, tiled=True)  68.1 us
    reduce_scatter x1, waiting for transfers between devices, reduce_late(): lax.psum_scatter(values[5], 'fsdp', scatter_dimension=0, tiled=True)  63.1 us
    ppermute x7, waiting for transfers between devices, positions_mark(): lax.ppermute(items[b - 1], 'fsdp', [(rr, (rr - 1) % devs) for rr in range...  46.7 us
    psum x1, blocking collectives, local(): lax.psum((jnp.sum(picked, axis=0), jnp.sum(picked * picked, axis=0)), ('d...  40.4 us
  transfers between devices with their start and end apart: 22, of which 17 were waited for; matrix products, arithmetic and copies ran while one was open for 13% of the time, Pallas kernels for 0%

profile of v1, /device:TPU:0, one launch (start us, length us, event | category | flops | bytes accessed | tf_op | source)
XLA Modules:
  0.0 1088.4 jit_solution(6493740700763325038)
XLA Ops:
  9.6 3.4 collective-permute-start
  13.5 5.0 collective-permute-done
  18.5 2.8 collective-permute-start.1
  24.7 31.0 %all-reduce.37 = (bf16[1280]{0:T(1024)(128)(2,1)S(1)}, bf16[1280]{0:T(1024)(128)(2,1)S(1)}, bf16[1280]{0:T(1024)(128)(2,1)S(1)}, bf16[1280]{0:T(1024)(128)(2,1)S...) all-reduce(bf16[1280]{0:T(1024)(128)(2,1)S(1)} %dynamic-update-slic, ...), channel_id=1, replica_groups=mesh['dp'=4,'fsdp'=8] {'fsdp'}, use_global_device_ids=true, to_apply=%add.1 | all-reduce | flops 10240 | bytes 40960
  55.8 8.0 all-gather
  64.0 1.4 collective-permute-start.2
  65.6 12.6 %collective-permute-done.2 = bf16[160,1280]{1,0:T(8,128)(2,1)S(1)} collective-permute-done((bf16[160,1280]{1,0:T(8,128)(2,1)S(1)}, bf16[160,1280]{1,0:T(8,128)(2,1)S(1)}, u32[]{:S(2)}, u32[]{:S(2)}) %collective-permute-start.2) | collective-permute-done | bytes 409632 | tf_op jit(solution)/shard_map/ppermute | solution.py:21
  78.2 2.9 collective-permute-start.3
  81.0 0.8 constant_dynamic-update-slice_fusion.15
  81.9 4.6 collective-permute-done.3
  86.5 2.8 collective-permute-start.4
  90.1 0.8 constant_dynamic-update-slice_fusion.13
  90.9 8.0 collective-permute-done.4
  98.9 2.9 collective-permute-start.5
  103.3 12.7 %collective-permute-done.5 = bf16[160,1280]{1,0:T(8,128)(2,1)S(1)} collective-permute-done((bf16[160,1280]{1,0:T(8,128)(2,1)S(1)}, bf16[160,1280]{1,0:T(8,128)(2,1)S(1)}, u32[]{:S(2)}, u32[]{:S(2)}) %collective-permute-start.5) | collective-permute-done | bytes 409632 | tf_op jit(solution)/shard_map/ppermute | solution.py:21
  116.0 2.9 collective-permute-start.6
  118.8 0.8 constant_dynamic-update-slice_fusion.10
  120.4 3.9 collective-permute-done.6
  126.6 0.8 constant_dynamic-update-slice_fusion.5
  128.2 0.8 constant_dynamic-update-slice_fusion.3
  131.4 5.4 fusion.74
  139.1 3.1 fusion.81
  142.4 21.7 %all-gather.11.cloned.1.call-done = bf16[1280,5120]{1,0:T(8,128)(2,1)} async-done(((bf16[160,5120]{1,0:T(8,128)(2,1)}), bf16[1280,5120]{1,0:T(8,128)(2,1)}) %all-gather.11.cloned.1.call-update) | async-done | bytes 13107216 | tf_op jit(solution)/shard_map/all_gather | solution.py:213
  164.2 8.2 convolution_add_fusion
  172.4 68.1 %all-gather.13.cloned.1.call-done = bf16[5120,1280]{1,0:T(8,128)(2,1)} async-done(((bf16[640,1280]{1,0:T(8,128)(2,1)}), bf16[5120,1280]{1,0:T(8,128)(2,1)}) %all-gather.13.cloned.1.call-update) | async-done | bytes 13107216 | tf_op jit(solution)/shard_map/all_gather | solution.py:215
  240.5 14.4 %convert_reduce_fusion = (f32[5120]{0:T(1024)S(1)}, bf16[128,5120]{1,0:T(8,128)(2,1)}, f32[128,5120]{1,0:T(8,128)}) fusion(f32[128,5120]{1,0:T(8,128)} %convolution_add_fusion, bf16[128,1280]{1,0:T(8,128)(2,1)} %param.33, bf16[5120,1280]{1,0:T(8,128)(2,1)} %all-gather.13.cloned.1.call-done), kind=kOutput, calls=%fused_computation.6 | convolution fusion | flops 1726213120 | bytes 20008960 | tf_op jit(solution)/shard_map/td,fd->tf/dot_general | solution.py:292
  254.9 6.6 multiply_reduce_fusion.2
  261.5 1.6 convert_reduce_fusion.3
  263.1 12.0 %all-gather.15.cloned.1.call-done = bf16[1280,1280]{1,0:T(8,128)(2,1)} async-done(((bf16[160,1280]{1,0:T(8,128)(2,1)}), bf16[1280,1280]{1,0:T(8,128)(2,1)}) %all-gather.15.cloned.1.call-update) | async-done | bytes 3276816 | tf_op jit(solution)/shard_map/all_gather | solution.py:280
  275.1 3.8 convolution_convert_fusion
  278.9 1.9 copy.66
  280.8 2.3 convert_reduce_fusion.4
  283.1 2.5 fusion.84
  285.6 3.1 fusion.31
  288.7 3.1 convert_reduce_fusion.5
  291.7 9.4 fusion.57
  301.2 1.2 copy-done.4
  302.4 15.4 %fusion.76 = f32[1280,5120]{1,0:T(8,128)} fusion(bf16[128,5120]{1,0:T(8,128)(2,1)S(1)} %copy-done.4, f32[128,1280]{1,0:T(8,128)S(1)} %get-tuple-element.82, f32[1280]{0:T(1024)S(1)} %convert_element_type.233, f32[1280]{0:T(1024)S(1)} %convert_element_type.232, f32[128]{0:T(128)S(1)} %add_rsqrt_fusion, f32[128]{0:T(128)S(1)} %broadcast_multiply_fusion.5), kind=kOutput, calls=%fused_computation.140 | convolution fusion | flops 1678540800 | bytes 28191744 | tf_op jit(solution)/shard_map/td,tf->df/dot_general | solution.py:295
  317.9 4.1 multiply_convert_fusion
  321.9 12.7 %fusion.85 = f32[5120,1280]{1,0:T(8,128)} fusion(bf16[128,5120]{1,0:T(8,128)(2,1)S(1)} %multiply_convert_fusion, bf16[128,1280]{1,0:T(8,128)(2,1)S(1)} %copy-done.10), kind=kOutput, calls=%fused_computation.146 | convolution fusion | flops 1677721600 | bytes 27852800 | tf_op jit(solution)/shard_map/tf,td->fd/dot_general | solution.py:291
  334.7 3.8 fusion.68
  338.6 92.4 %reduce-scatter.9.cloned.1.call-done = f32[160,3840]{1,0:T(8,128)} async-done(((f32[1280,3840]{1,0:T(8,128)}), f32[160,3840]{1,0:T(8,128)}) %reduce-scatter.9.cloned.1.call-update) | async-done | bytes 2457616 | tf_op jit(solution)/shard_map/reduce_scatter | solution.py:68
  430.9 2.8 convert_element_type.254
  433.9 163.0 %reduce-scatter.17.cloned.1.call-done = f32[160,5120]{1,0:T(8,128)} async-done(((f32[1280,5120]{1,0:T(8,128)}), f32[160,5120]{1,0:T(8,128)}) %reduce-scatter.17.cloned.1.call-update) | async-done | bytes 3276816 | tf_op jit(solution)/shard_map/reduce_scatter | solution.py:75
  596.9 3.3 convert_element_type.271
  600.2 162.7 %reduce-scatter.21.cloned.1.call-done = f32[640,1280]{1,0:T(8,128)} async-done(((f32[5120,1280]{1,0:T(8,128)}), f32[640,1280]{1,0:T(8,128)}) %reduce-scatter.21.cloned.1.call-update) | async-done | bytes 3276816 | tf_op jit(solution)/shard_map/reduce_scatter | solution.py:77
  762.9 3.2 convert_element_type.276
  766.3 63.1 %reduce-scatter.13.cloned.1.call-done = f32[160,1280]{1,0:T(8,128)} async-done(((f32[1280,1280]{1,0:T(8,128)}), f32[160,1280]{1,0:T(8,128)}) %reduce-scatter.13.cloned.1.call-update) | async-done | bytes 819216 | tf_op jit(solution)/shard_map/reduce_scatter | solution.py:71
  829.4 1.9 convert_element_type.262
  831.4 31.1 %reduce-scatter.11.cloned.1.call-done = bf16[40,3840]{1,0:T(8,128)(2,1)} async-done(((bf16[160,3840]{1,0:T(8,128)(2,1)}), bf16[40,3840]{1,0:T(8,128)(2,1)}) %reduce-scatter.11.cloned.1.call-update) | async-done | bytes 307216 | tf_op jit(solution)/shard_map/reduce_scatter | solution.py:87
  862.6 37.7 %reduce-scatter.19.cloned.1.call-done = bf16[40,5120]{1,0:T(8,128)(2,1)} async-done(((bf16[160,5120]{1,0:T(8,128)(2,1)}), bf16[40,5120]{1,0:T(8,128)(2,1)}) %reduce-scatter.19.cloned.1.call-update) | async-done | bytes 409616 | tf_op jit(solution)/shard_map/reduce_scatter | solution.py:108
  904.3 34.4 %reduce-scatter.23.cloned.1.call-done = bf16[160,1280]{1,0:T(8,128)(2,1)} async-done(((bf16[640,1280]{1,0:T(8,128)(2,1)}), bf16[160,1280]{1,0:T(8,128)(2,1)}) %reduce-scatter.23.cloned.1.call-update) | async-done | bytes 409616 | tf_op jit(solution)/shard_map/reduce_scatter | solution.py:114
  938.8 8.2 fusion.47
  947.2 25.2 %all-reduce.36 = (bf16[1280]{0:T(1024)(128)(2,1)S(1)}, bf16[1280]{0:T(1024)(128)(2,1)S(1)}, bf16[1280]{0:T(1024)(128)(2,1)S(1)}, bf16[1280]{0:T(1024)(128)(2,1)S...) all-reduce(f32[1280]{0:T(1024)S(1)} %get-tuple-element.19, ...), channel_id=2, replica_groups=mesh['dp'=4,'fsdp'=8] {'fsdp'}, use_global_device_ids=true, to_apply=%region_15.16.clone | all-reduce | flops 15360 | bytes 92160
  973.0 10.7 all-reduce.39
  986.4 9.6 all-reduce.38
  1001.1 7.6 multiply_reduce_fusion.1
  1008.7 40.4 %all-reduce.35 = (f32[1280]{0:T(1024)S(1)}, f32[1280]{0:T(1024)S(1)}) all-reduce(f32[1280]{0:T(1024)S(1)} %get-tuple-element.24, f32[1280]{0:T(1024)S(1)} %get-tuple-element.23), channel_id=1, replica_groups=mesh['dp'=4,'fsdp'=8] {'dp','fsdp'}, use_global_device_ids=true, to_apply=%region_50.51 | all-reduce | flops 2560 | bytes 20480 | tf_op jit(solution)/shard_map/psum | solution.py:254
  1049.7 2.2 fusion.46
  1051.9 18.6 %all_gather.101 = bf16[160,1280]{1,0:T(8,128)(2,1)S(1)} all-gather(bf16[40,1280]{1,0:T(8,128)(2,1)} %reduce-scatter.15.cloned.1.call-done), channel_id=1, replica_groups=mesh['dp'=4,'fsdp'=8] {'dp'}, dimensions={0}, use_global_device_ids=true | all-gather | bytes 512000 | tf_op jit(solution)/shard_map/all_gather | solution.py:137
  1070.4 0.9 convert_element_type.263
  1071.4 2.9 convert_element_type.255
  1074.3 3.5 convert_element_type.272
  1078.2 3.4 convert_element_type.277
  (197 shorter events, 27.1 us)
Async XLA Ops:
  7.2 2.4 copy-start.5
  7.2 14.2 %copy-start.12 = (u32[32]{0:T(128)S(1)}, u32[32]{0:T(128)}, u32[]{:S(2)}) copy-start(u32[32]{0:T(128)} %constant.160) | copy-start | bytes 388
  7.2 14.2 %copy-start.13 = (u32[32]{0:T(128)S(1)}, u32[32]{0:T(128)}, u32[]{:S(2)}) copy-start(u32[32]{0:T(128)} %constant.120) | copy-start | bytes 388
  7.2 5.9 copy-start.15
  7.2 6.1 copy-start.3
  7.2 15.4 %copy-start.16 = (bf16[160]{0:T(256)(128)(2,1)S(1)}, bf16[160]{0:T(256)(128)(2,1)}, u32[]{:S(2)}) copy-start(bf16[160]{0:T(256)(128)(2,1)} %param.21) | copy-start | bytes 964
  7.3 15.7 %copy-start.17 = (bf16[160]{0:T(256)(128)(2,1)S(1)}, bf16[160]{0:T(256)(128)(2,1)}, u32[]{:S(2)}) copy-start(bf16[160]{0:T(256)(128)(2,1)} %param.20) | copy-start | bytes 964
  7.3 15.9 %copy-start.18 = (bf16[160]{0:T(256)(128)(2,1)S(1)}, bf16[160]{0:T(256)(128)(2,1)}, u32[]{:S(2)}) copy-start(bf16[160]{0:T(256)(128)(2,1)} %param.24) | copy-start | bytes 964
  7.3 16.2 %copy-start.19 = (bf16[160]{0:T(256)(128)(2,1)S(1)}, bf16[160]{0:T(256)(128)(2,1)}, u32[]{:S(2)}) copy-start(bf16[160]{0:T(256)(128)(2,1)} %param.23) | copy-start | bytes 964
  7.3 16.4 %copy-start.20 = (bf16[160]{0:T(256)(128)(2,1)S(1)}, bf16[160]{0:T(256)(128)(2,1)}, u32[]{:S(2)}) copy-start(bf16[160]{0:T(256)(128)(2,1)} %param.26) | copy-start | bytes 964
  7.3 16.6 %copy-start.21 = (bf16[160]{0:T(256)(128)(2,1)S(1)}, bf16[160]{0:T(256)(128)(2,1)}, u32[]{:S(2)}) copy-start(bf16[160]{0:T(256)(128)(2,1)} %param.28) | copy-start | bytes 964
  7.3 16.9 %copy-start.22 = (bf16[160]{0:T(256)(128)(2,1)S(1)}, bf16[160]{0:T(256)(128)(2,1)}, u32[]{:S(2)}) copy-start(bf16[160]{0:T(256)(128)(2,1)} %param.27) | copy-start | bytes 964
  7.3 17.1 %copy-start.23 = (bf16[160]{0:T(256)(128)(2,1)S(1)}, bf16[160]{0:T(256)(128)(2,1)}, u32[]{:S(2)}) copy-start(bf16[160]{0:T(256)(128)(2,1)} %param.32) | copy-start | bytes 964
  7.3 48.4 %copy-start.14 = (bf16[640]{0:T(1024)(128)(2,1)S(1)}, bf16[640]{0:T(1024)(128)(2,1)}, u32[]{:S(2)}) copy-start(bf16[640]{0:T(1024)(128)(2,1)} %param.30) | copy-start | bytes 3844
  7.3 124.0 %all-gather.9.cloned.1.call-start = ((), (), s32[]{:S(2)}) async-start(), calls=%async_computation.8 | async-start | bytes 11059200 | tf_op jit(solution)/shard_map/all_gather | solution.py:206
  8.1 57.4 %copy-start.24 = (s32[128]{0:T(128)S(1)}, s32[128]{0:T(128)}, u32[]{:S(2)}) copy-start(s32[128]{0:T(128)} %param.19) | copy-start | bytes 1540
  8.1 72.9 %copy-start.6 = (bf16[160,1280]{1,0:T(8,128)(2,1)S(1)}, bf16[160,1280]{1,0:T(8,128)(2,1)}, u32[]{:S(2)}) copy-start(bf16[160,1280]{1,0:T(8,128)(2,1)} %param.25) | copy-start | bytes 1228804
  8.1 156.1 %all-gather.11.cloned.1.call-start = ((), (), s32[]{:S(2)}) async-start(), calls=%async_computation.9 | async-start | bytes 14745600 | tf_op jit(solution)/shard_map/all_gather | solution.py:213
  8.8 231.6 %all-gather.13.cloned.1.call-start = ((), (), s32[]{:S(2)}) async-start(), calls=%async_computation.10 | async-start | bytes 14745600 | tf_op jit(solution)/shard_map/all_gather | solution.py:215
  9.6 265.5 %all-gather.15.cloned.1.call-start = ((), (), s32[]{:S(2)}) async-start(), calls=%async_computation.11 | async-start | bytes 3686400 | tf_op jit(solution)/shard_map/all_gather | solution.py:280
  9.6 8.9 collective-permute-start
  13.0 417.9 %reduce-scatter.9.cloned.1.call-start = ((), (), s32[]{:S(2)}) async-start(), calls=%async_computation.12 | async-start | bytes 22118400 | tf_op jit(solution)/shard_map/reduce_scatter | solution.py:68
  18.5 45.5 %collective-permute-start.1 = (bf16[160,1280]{1,0:T(8,128)(2,1)S(1)}, bf16[160,1280]{1,0:T(8,128)(2,1)S(1)}, u32[]{:S(2)}, u32[]{:S(2)}) collective-permute-start(bf16[160,1280]{1,0:T(8,128)(2,1)S(1)} %collective-permute-done), channel_id=1, source_target_pairs={{0,7},{1,0},{2,1},{3,2},{4,3},{5,4},{6,5},{7,6},{8,15},{9,8},{10,9... | collective-permute-start | bytes 1228808 | tf_op jit(solution)/shard_map/ppermute | solution.py:21
  64.0 14.1 %collective-permute-start.2 = (bf16[160,1280]{1,0:T(8,128)(2,1)S(1)}, bf16[160,1280]{1,0:T(8,128)(2,1)S(1)}, u32[]{:S(2)}, u32[]{:S(2)}) collective-permute-start(bf16[160,1280]{1,0:T(8,128)(2,1)S(1)} %collective-permute-done.1), channel_id=1, source_target_pairs={{0,7},{1,0},{2,1},{3,2},{4,3},{5,4},{6,5},{7,6},{8,15},{9,8},{10,9... | collective-permute-start | bytes 1228808 | tf_op jit(solution)/shard_map/ppermute | solution.py:21
  78.2 8.3 collective-permute-start.3
  86.5 12.4 %collective-permute-start.4 = (bf16[160,1280]{1,0:T(8,128)(2,1)S(1)}, bf16[160,1280]{1,0:T(8,128)(2,1)S(1)}, u32[]{:S(2)}, u32[]{:S(2)}) collective-permute-start(bf16[160,1280]{1,0:T(8,128)(2,1)S(1)} %collective-permute-done.3), channel_id=1, source_target_pairs={{0,7},{1,0},{2,1},{3,2},{4,3},{5,4},{6,5},{7,6},{8,15},{9,8},{10,9... | collective-permute-start | bytes 1228808 | tf_op jit(solution)/shard_map/ppermute | solution.py:21
  98.9 17.1 %collective-permute-start.5 = (bf16[160,1280]{1,0:T(8,128)(2,1)S(1)}, bf16[160,1280]{1,0:T(8,128)(2,1)S(1)}, u32[]{:S(2)}, u32[]{:S(2)}) collective-permute-start(bf16[160,1280]{1,0:T(8,128)(2,1)S(1)} %collective-permute-done.4), channel_id=1, source_target_pairs={{0,7},{1,0},{2,1},{3,2},{4,3},{5,4},{6,5},{7,6},{8,15},{9,8},{10,9... | collective-permute-start | bytes 1228808 | tf_op jit(solution)/shard_map/ppermute | solution.py:21
  116.0 8.3 collective-permute-start.6
  137.1 1.4 copy-start.7
  137.3 1.2 copy-start.9
  137.6 1.0 copy-start.8
  138.0 1.1 copy-start.1
  240.5 14.4 %copy-start = (bf16[1280,5120]{1,0:T(8,128)(2,1)S(1)}, bf16[1280,5120]{1,0:T(8,128)(2,1)}, u32[]{:S(2)}) copy-start(bf16[1280,5120]{1,0:T(8,128)(2,1)} %all-gather.11.cloned.1.call-done) | copy-start | bytes 39321604
  263.1 17.7 %copy-start.2 = (f32[20,128,128]{1,2,0:T(8,128)S(1)}, f32[20,128,128]{1,2,0:T(8,128)}, u32[]{:S(2)}) copy-start(f32[20,128,128]{1,2,0:T(8,128)} %copy-done.1) | copy-start | bytes 3932164
  301.1 1.3 copy-start.4
  301.1 295.7 %reduce-scatter.17.cloned.1.call-start = ((), (), s32[]{:S(2)}) async-start(), calls=%async_computation.17 | async-start | bytes 29491200 | tf_op jit(solution)/shard_map/reduce_scatter | solution.py:75
  317.8 445.1 %reduce-scatter.21.cloned.1.call-start = ((), (), s32[]{:S(2)}) async-start(), calls=%async_computation.20 | async-start | bytes 29491200 | tf_op jit(solution)/shard_map/reduce_scatter | solution.py:77
  317.8 4.1 copy-start.10
  334.6 494.8 %reduce-scatter.13.cloned.1.call-start = ((), (), s32[]{:S(2)}) async-start(), calls=%async_computation.15 | async-start | bytes 7372800 | tf_op jit(solution)/shard_map/reduce_scatter | solution.py:71
  338.5 524.0 %reduce-scatter.11.cloned.1.call-start = ((), (), s32[]{:S(2)}) async-start(), calls=%async_computation.13 | async-start | bytes 1536000 | tf_op jit(solution)/shard_map/reduce_scatter | solution.py:87
  433.8 466.6 %reduce-scatter.19.cloned.1.call-start = ((), (), s32[]{:S(2)}) async-start(), calls=%async_computation.18 | async-start | bytes 2048000 | tf_op jit(solution)/shard_map/reduce_scatter | solution.py:108
  600.2 338.6 %reduce-scatter.23.cloned.1.call-start = ((), (), s32[]{:S(2)}) async-start(), calls=%async_computation.21 | async-start | bytes 2048000 | tf_op jit(solution)/shard_map/reduce_scatter | solution.py:114
  766.2 172.6 %copy-start.11 = (bf16[20,64,128]{2,1,0:T(8,128)(2,1)S(1)}, bf16[20,64,128]{2,1,0:T(8,128)(2,1)}, u32[]{:S(2)}) copy-start(bf16[20,64,128]{2,1,0:T(8,128)(2,1)} %get-tuple-element.89) | copy-start | bytes 983044
  766.2 285.7 %reduce-scatter.15.cloned.1.call-start = ((), (), s32[]{:S(2)}) async-start(), calls=%async_computation.16 | async-start | bytes 512000 | tf_op jit(solution)/shard_map/reduce_scatter | solution.py:96
  831.4 240.0 %all-gather.17.cloned.1.call-start = ((), (), s32[]{:S(2)}) async-start(), calls=%async_computation.14 | async-start | bytes 1536000 | tf_op jit(solution)/shard_map/all_gather | solution.py:128
  862.6 211.7 %all-gather.19.cloned.1.call-start = ((), (), s32[]{:S(2)}) async-start(), calls=%async_computation.19 | async-start | bytes 2048000 | tf_op jit(solution)/shard_map/all_gather | solution.py:149
  900.4 177.8 %all-gather.21.cloned.1.call-start = ((), (), s32[]{:S(2)}) async-start(), calls=%async_computation.22 | async-start | bytes 2048000 | tf_op jit(solution)/shard_map/all_gather | solution.py:155
Sparse Core Ops, SparseCore 0:
  10.1 71.7 all-gather.8
  83.7 80.3 all-gather.10
  166.1 74.3 all-gather.12
  242.2 32.8 all-gather.14
  301.2 129.6 reduce-scatter.8
  434.5 162.3 reduce-scatter.16
  600.6 162.3 reduce-scatter.20
  766.4 62.9 reduce-scatter.12
  832.4 30.0 reduce-scatter.10
  865.3 35.0 reduce-scatter.18
  903.4 35.3 reduce-scatter.22
  941.5 19.7 reduce-scatter.14
  962.9 30.5 all-gather.16
  995.0 37.9 all-gather.18
  1034.5 43.6 all-gather.20
